TPU v7x, 32 devices: a whole 2x2x4 slice. The times are simulated.
32 devices in a mesh: req: 4 (over z), seq: 8 (over y, x, core).
Axes of the slice: x: 2, y: 2, z: 4, core: 2. Of those that a mesh axis runs over, the one named last changes fastest.
Arguments:
- hidden_in: bfloat16 [4, 32, 4, 2048], P(None, 'req', None, 'seq'), may hold values from -30 to 30
- cache_lens: int32 [32], P('req'), may hold values from 1 to 4092, as said below
- page_table: int32 [32, 32], P('req'), may hold values from -1 to 55, as said below
- key_cache: bfloat16 [224, 128, 1024], P(('req', 'seq')), may hold values from -250 to 250
- value_cache: bfloat16 [224, 128, 1024], P(('req', 'seq')), may hold values from -4 to 4
- norm_attn: float32 [8192], replicated, may hold values from 0.1 to 1.9
- w_qkv: bfloat16 [8192, 10240], P(None, 'seq'), may hold values from -0.0625 to 0.0625
- b_qkv: bfloat16 [10240], P('seq'), may hold values from -3 to 3
- w_out: bfloat16 [8192, 4, 2048], P(None, None, 'seq'), may hold values from -0.25 to 0.25
- norm_mlp: float32 [8192], replicated, may hold values from 0.1 to 1.9
- w_gate: bfloat16 [8192, 29568], P('req', 'seq'), may hold values from -0.0625 to 0.0625
- w_up: bfloat16 [8192, 29568], P('req', 'seq'), may hold values from -0.0625 to 0.0625
- w_down: bfloat16 [29568, 8192], P('seq', 'req'), may hold values from -0.03125 to 0.03125
Outputs:
- hidden_out: bfloat16 [4, 32, 4, 2048], P(None, 'req', None, 'seq')
- key_cache_out: bfloat16 [224, 128, 1024], P(('req', 'seq'))
- value_cache_out: bfloat16 [224, 128, 1024], P(('req', 'seq'))
Inputs may be any that keep to these rules, and one draw needn't show every extreme that they name: `cache_lens`: in each group of 8 requests exactly one holds 4092 tokens and one holds 380; every other one holds at most 380. For request r and logical page j below ceil((cache_lens[r]+4)/128), page_table[r, j] is a slot of the group's 56 page slots (slot s*7+p is the p-th slot of seq index s); no slot is named twice within a group; all other entries are -1.
All inputs are finite; a program needn't handle non-finite values.
Results may differ from a plain program's by a relative error of at most 0.012.
The roundings to bfloat16 on the way count: a program that leaves them out, or rounds other values in their place, can miss the bound.
Values may be sent and summed in bfloat16 or wider, within the bound.
A program may use at most 320 MiB of HBM per device.

v0:
```python
import math

import jax
import jax.numpy as jnp
from jax import lax
from jax.sharding import PartitionSpec as P

D = 8192
H = 64
KV = 8
HD = 128
STEPS = 4


EPSILON = 1e-06
THETA = 1000000.0
NEGATIVE = -1e30


def rotate(heads, position):
    half = heads.shape[-1] // 2
    freq = THETA ** (-(jnp.arange(half, dtype=jnp.float32) * 2.0 / heads.shape[-1]))
    angle = position.astype(jnp.float32)[:, None, None] * freq[None, None, :]
    cosine = jnp.cos(angle)
    sine = jnp.sin(angle)
    first = heads[..., :half]
    second = heads[..., half:]
    return jnp.concatenate(
        [first * cosine - second * sine, second * cosine + first * sine], axis=-1
    )


def on_device(
    hidden_in,
    cache_lens,
    page_table,
    key_cache,
    value_cache,
    norm_attn,
    w_qkv,
    b_qkv,
    w_out,
    norm_mlp,
    w_gate,
    w_up,
    w_down,
):
    steps, requests, blocks, pieces = hidden_in.shape
    rows = steps * requests
    slots, per_page, _ = key_cache.shape
    group = H // KV
    quarter = D // blocks
    seq = quarter // pieces
    scale = 1.0 / math.sqrt(HD)
    slot_ids = lax.axis_index("seq") * slots + jnp.arange(slots, dtype=jnp.int32)
    matches = page_table[:, :, None] == slot_ids[None, None, :]
    live = jnp.any(matches, axis=(0, 1))
    owner = jnp.sum(
        jnp.where(matches, jnp.arange(requests, dtype=jnp.int32)[:, None, None], 0), axis=(0, 1)
    )
    logical = jnp.sum(
        jnp.where(matches, jnp.arange(page_table.shape[1], dtype=jnp.int32)[None, :, None], 0),
        axis=(0, 1),
    )
    owned = jnp.logical_and(
        jnp.arange(requests, dtype=jnp.int32)[None, :] == owner[:, None], live[:, None]
    )
    slot_length = jnp.sum(jnp.where(owned, cache_lens[None, :], 0), axis=1)
    positions = logical[:, None] * per_page + jnp.arange(per_page, dtype=jnp.int32)[None, :]

    flat = (
        lax.all_gather(hidden_in, "seq", axis=3, tiled=True).reshape(rows, D).astype(jnp.float32)
    )
    normed = (
        flat * lax.rsqrt(jnp.mean(flat * flat, axis=1, keepdims=True) + EPSILON) * norm_attn
    ).astype(jnp.bfloat16)
    columns = (
        jnp.dot(normed, w_qkv, preferred_element_type=jnp.float32) + b_qkv.astype(jnp.float32)
    ).astype(jnp.bfloat16)
    projected = lax.all_gather(columns, "seq", axis=1, tiled=True)
    position = (
        jnp.arange(steps, dtype=jnp.int32)[:, None] + cache_lens[None, :]
    ).reshape(rows)
    rotated = rotate(
        projected[:, : (H + KV) * HD].reshape(rows, H + KV, HD).astype(jnp.float32), position
    ).astype(jnp.bfloat16)
    queries = rotated[:, :H].reshape(steps, requests, KV, group, HD)
    new_keys = rotated[:, H:].reshape(steps, requests, KV * HD)
    new_values = projected[:, (H + KV) * HD :].reshape(steps, requests, KV * HD)
    slot_keys = jnp.take(new_keys, owner, axis=1)
    slot_values = jnp.take(new_values, owner, axis=1)
    for step in range(steps):
        write_here = jnp.logical_and(live[:, None], positions == (slot_length + step)[:, None])[
            :, :, None
        ]
        key_cache = jnp.where(write_here, slot_keys[step][:, None, :], key_cache)
        value_cache = jnp.where(write_here, slot_values[step][:, None, :], value_cache)

    slot_queries = jnp.take(queries, owner, axis=1)
    keys_view = key_cache.reshape(slots, per_page, KV, HD)
    values_view = value_cache.reshape(slots, per_page, KV, HD)
    scores = (
        jnp.einsum("tjkgd,jpkd->jktgp", slot_queries, keys_view, preferred_element_type=jnp.float32)
        * scale
    )
    last = slot_length[:, None] + jnp.arange(steps, dtype=jnp.int32)[None, :]
    valid = jnp.logical_and(
        live[:, None, None], positions[:, None, :] <= last[:, :, None]
    )[:, None, :, None, :]
    masked = jnp.where(valid, scores, NEGATIVE)
    page_max = jnp.max(masked, axis=4)
    weights = jnp.where(valid, jnp.exp(masked - page_max[..., None]), 0.0).astype(jnp.bfloat16)
    page_sum = jnp.sum(weights.astype(jnp.float32), axis=4)
    page_acc = jnp.einsum(
        "jktgp,jpkd->jktgd", weights, values_view, preferred_element_type=jnp.float32
    )
    spread = owned[:, :, None, None, None]
    candidates = jnp.where(spread, page_max[:, None], NEGATIVE)
    top = jnp.max(candidates, axis=0)
    factor = jnp.where(spread, jnp.exp(candidates - top[None]), 0.0)
    total = jnp.sum(factor * page_sum[:, None], axis=0)
    summed = jnp.sum(factor[..., None] * page_acc[:, None], axis=0)
    def by_head(value):
        value = jnp.moveaxis(value, 0, 3)
        value = jnp.swapaxes(value, 1, 2)
        return value.reshape((seq, H // seq, rows) + value.shape[4:])

    packed = jnp.concatenate(
        [
            by_head(summed).reshape(seq, -1),
            by_head(top).reshape(seq, -1),
            by_head(total).reshape(seq, -1),
        ],
        axis=1,
    )
    packed = lax.all_to_all(packed, "seq", split_axis=0, concat_axis=0, tiled=True)
    count = (H // seq) * rows
    part_acc = packed[:, : count * HD].reshape(seq, count, HD)
    part_top = packed[:, count * HD : count * (HD + 1)]
    part_sum = packed[:, count * (HD + 1) :]
    best = jnp.max(part_top, axis=0)
    share = jnp.exp(part_top - best[None])
    denominator = jnp.sum(share * part_sum, axis=0)
    numerator = jnp.sum(share[..., None] * part_acc, axis=0)
    heads = (numerator / denominator[:, None]).astype(jnp.bfloat16)
    heads = jnp.swapaxes(heads.reshape(H // seq, rows, HD), 0, 1).reshape(rows, -1)
    attended = lax.all_gather(heads, "seq", axis=1, tiled=True)
    branch_out = jnp.dot(
        attended, w_out.reshape(H * HD, blocks * pieces), preferred_element_type=jnp.float32
    ).reshape(rows, blocks, pieces)
    current = hidden_in.reshape(rows, blocks, pieces).astype(jnp.float32)
    middle = (current + branch_out).astype(jnp.bfloat16)
    rows_mid = lax.all_gather(middle, "seq", axis=2, tiled=True).astype(jnp.float32)
    inverse = lax.rsqrt(jnp.mean(rows_mid * rows_mid, axis=(1, 2), keepdims=True) + EPSILON)
    normed_mid = (rows_mid * inverse * norm_mlp.reshape(blocks, quarter)).astype(jnp.bfloat16)
    mine = lax.all_to_all(normed_mid, "req", split_axis=1, concat_axis=0, tiled=True).reshape(
        -1, quarter
    )
    gate_part = jnp.dot(mine, w_gate, preferred_element_type=jnp.float32).astype(jnp.bfloat16)
    up_part = jnp.dot(mine, w_up, preferred_element_type=jnp.float32).astype(jnp.bfloat16)
    gate_sum = lax.psum_scatter(gate_part, "req", scatter_dimension=0, tiled=True)
    up_sum = lax.psum_scatter(up_part, "req", scatter_dimension=0, tiled=True)
    hidden_part = (
        jax.nn.silu(gate_sum.astype(jnp.float32)) * up_sum.astype(jnp.float32)
    ).astype(jnp.bfloat16)
    hidden = lax.all_gather(hidden_part, "req", axis=0, tiled=True)
    down = jnp.dot(hidden, w_down, preferred_element_type=jnp.float32)
    sums = lax.psum_scatter(
        down.reshape(down.shape[0], 1, quarter).astype(jnp.bfloat16),
        "seq",
        scatter_dimension=2,
        tiled=True,
    ).astype(jnp.float32)
    back = lax.all_to_all(sums, "req", split_axis=0, concat_axis=1, tiled=True)
    output = (middle.astype(jnp.float32) + back).astype(jnp.bfloat16)
    return (output.reshape(hidden_in.shape), key_cache, value_cache)


def solution(mesh):
    in_specs = (
        P(None, "req", None, "seq"),
        P("req"),
        P("req", None),
        P(("req", "seq"), None, None),
        P(("req", "seq"), None, None),
        P(),
        P(None, "seq"),
        P("seq"),
        P(None, None, "seq"),
        P(),
        P("req", "seq"),
        P("req", "seq"),
        P("seq", "req"),
    )
    out_specs = (
        P(None, "req", None, "seq"),
        P(("req", "seq"), None, None),
        P(("req", "seq"), None, None),
    )
    return jax.shard_map(
        on_device, mesh=mesh, in_specs=in_specs, out_specs=out_specs, check_vma=False
    )
```

profile of v0, /device:TPU:0, one launch (start us, length us, event | category | flops | bytes accessed | tf_op | source)
XLA Modules:
  0.0 303.2 jit_solution(10138137191504181131)
XLA Ops:
  9.3 11.7 %all_gather.15 = bf16[4,8,4,2048]{3,2,1,0:T(4,128)(2,1)S(1)} all-gather(bf16[4,8,4,256]{3,2,1,0:T(4,128)(2,1)} %param.15), channel_id=1, replica_groups=mesh['req'=4,'seq'=8] {'seq'}, dimensions={3}, use_global_device_ids=true | all-gather | bytes 589824 | tf_op jit(solution)/shard_map/all_gather | solution.py:72
  22.2 9.0 %fusion.1 = bf16[32,1280]{1,0:T(8,128)(2,1)S(1)} fusion(bf16[8192,1280]{1,0:T(8,128)(2,1)} %param.21, f32[32,8192]{1,0:T(8,128)S(1)} %bitcast.124, f32[8192]{0:T(1024)S(1)} %copy-done.5, f32[32]{0:T(128)S(1)} %rsqrt.20, f32[1280]{0:T(1024)S(1)} %convert_element_type.96), kind=kOutput, calls=%fused_computation.9 | convolution fusion | flops 671956992 | bytes 22140032 | tf_op jit(solution)/shard_map/dot_general | solution.py:78
  31.2 10.3 %all_gather.16 = bf16[32,10240]{1,0:T(8,128)(2,1)S(1)} all-gather(bf16[32,1280]{1,0:T(8,128)(2,1)S(1)} %fusion.1), channel_id=1, replica_groups=mesh['req'=4,'seq'=8] {'seq'}, dimensions={1}, use_global_device_ids=true | all-gather | bytes 737280 | tf_op jit(solution)/shard_map/all_gather | solution.py:80
  45.7 2.8 select_select_fusion
  49.7 1.4 bitcast_bitcast_fusion.1
  51.8 2.7 fusion.48
  59.1 2.3 multiply_reduce_fusion
  62.7 2.1 copy.101
  64.8 3.6 %all-to-all-start = ((f32[8,1,33280]{2,1,0:T(1,128)}), f32[8,1,33280]{2,1,0:T(1,128)S(1)}, u32[]{:S(2)}, u32[]{:S(2)}) async-start(f32[8,1,33280]{2,1,0:T(1,128)} %copy.101), calls=%async_computation | async-start | bytes 2129920 | tf_op jit(solution)/shard_map/all_to_all | solution.py:136
  68.6 16.8 %copy.129 = bf16[1024,8,4,256]{3,1,2,0:T(8,128)(2,1)} copy(bf16[1024,8,4,256]{3,2,1,0:T(4,128)(2,1)} %bitcast.118) | data formatting | bytes 33554432
  85.4 20.9 %copy.104 = bf16[1024,8192]{1,0:T(8,128)(2,1)} copy(bf16[1024,8192]{0,1:T(8,128)(2,1)} %bitcast.117) | data formatting | bytes 33554432 | tf_op jit(solution)/shard_map/dot_general | solution.py:148
  107.2 10.0 %all_gather.17 = bf16[32,8192]{1,0:T(8,128)(2,1)S(1)} all-gather(bf16[32,1024]{1,0:T(8,128)(2,1)S(1)} %copy_bitcast_fusion.2), channel_id=1, replica_groups=mesh['req'=4,'seq'=8] {'seq'}, dimensions={1}, use_global_device_ids=true | all-gather | bytes 589824 | tf_op jit(solution)/shard_map/all_gather | solution.py:147
  117.2 10.8 %fusion.12 = bf16[32,4,256]{2,0,1:T(8,128)(2,1)S(1)} fusion(bf16[4,256,8192]{2,1,0:T(8,128)(2,1)} %bitcast.116, bf16[32,8192]{1,0:T(8,128)(2,1)S(1)} %all_gather.17, f32[4,8,4,256]{3,2,1,0:T(4,128)S(1)} %convert_element_type.118), kind=kOutput, calls=%fused_computation.30 | convolution fusion | flops 536936448 | bytes 17498112 | tf_op jit(solution)/shard_map/dot_general | solution.py:148
  128.0 11.2 %all_gather.18 = bf16[32,4,2048]{2,0,1:T(8,128)(2,1)S(1)} all-gather(bf16[32,4,256]{2,0,1:T(8,128)(2,1)S(1)} %fusion.12), channel_id=1, replica_groups=mesh['req'=4,'seq'=8] {'seq'}, dimensions={2}, use_global_device_ids=true | all-gather | bytes 589824 | tf_op jit(solution)/shard_map/all_gather | solution.py:153
  139.7 19.7 %all_to_all.45 = bf16[32,4,2048]{2,0,1:T(8,128)(2,1)S(1)} all-to-all(bf16[32,4,2048]{2,0,1:T(8,128)(2,1)S(1)} %fusion.15), channel_id=1, replica_groups=mesh['req'=4,'seq'=8] {'req'}, dimensions={1} | all-to-all | bytes 1048576 | tf_op jit(solution)/shard_map/all_to_all | solution.py:156
  159.4 11.3 %convolution_convert_fusion = bf16[128,3696]{1,0:T(8,128)(2,1)} fusion(bf16[128,2048]{1,0:T(8,128)(2,1)S(1)} %bitcast.125, bf16[2048,3696]{0,1:T(8,128)(2,1)} %param.26), kind=kOutput, calls=%fused_computation.4 | convolution fusion | flops 1938241536 | bytes 16609280 | tf_op jit(solution)/shard_map/dot_general | solution.py:160
  171.0 11.5 %convolution_convert_fusion.1 = bf16[128,3696]{1,0:T(8,128)(2,1)} fusion(bf16[128,2048]{1,0:T(8,128)(2,1)S(1)} %bitcast.126, bf16[2048,3696]{0,1:T(8,128)(2,1)} %param.25), kind=kOutput, calls=%fused_computation.5 | convolution fusion | flops 1938241536 | bytes 16609280 | tf_op jit(solution)/shard_map/dot_general | solution.py:159
  182.6 12.0 %reduce-scatter.6.cloned.1.call-done = bf16[32,3696]{1,0:T(8,128)(2,1)} async-done(((bf16[128,3696]{1,0:T(8,128)(2,1)}), bf16[32,3696]{1,0:T(8,128)(2,1)}) %reduce-scatter.6.cloned.1.call-update) | async-done | bytes 236560 | tf_op jit(solution)/shard_map/reduce_scatter | solution.py:162
  194.6 26.8 %reduce-scatter.4.cloned.1.call-done = bf16[32,3696]{1,0:T(8,128)(2,1)} async-done(((bf16[128,3696]{1,0:T(8,128)(2,1)}), bf16[32,3696]{1,0:T(8,128)(2,1)}) %reduce-scatter.4.cloned.1.call-update) | async-done | bytes 236560 | tf_op jit(solution)/shard_map/reduce_scatter | solution.py:161
  221.4 1.2 fusion.28
  222.6 19.6 %all_gather.19 = bf16[128,3696]{1,0:T(8,128)(2,1)S(1)} all-gather(bf16[32,3696]{1,0:T(8,128)(2,1)S(1)} %fusion.28), channel_id=1, replica_groups=mesh['req'=4,'seq'=8] {'req'}, dimensions={0}, use_global_device_ids=true | all-gather | bytes 1182720 | tf_op jit(solution)/shard_map/all_gather | solution.py:166
  242.3 8.5 %fusion = bf16[128,1,2048]{2,0,1:T(8,128)(2,1)} fusion(bf16[128,3696]{1,0:T(8,128)(2,1)S(1)} %all_gather.19, bf16[3696,2048]{1,0:T(8,128)(2,1)} %param.27), kind=kOutput, calls=%fused_computation.7 | convolution fusion | flops 1938030592 | bytes 16609280 | tf_op jit(solution)/shard_map/dot_general | solution.py:167
  250.8 33.8 %reduce-scatter.8.cloned.1.call-done = bf16[128,1,256]{2,0,1:T(8,128)(2,1)} async-done(((bf16[128,1,2048]{2,0,1:T(8,128)(2,1)}), bf16[128,1,256]{2,0,1:T(8,128)(2,1)}) %reduce-scatter.8.cloned.1.call-update) | async-done | bytes 65552 | tf_op jit(solution)/shard_map/reduce_scatter | solution.py:168
  285.6 10.3 %all_to_all.46 = f32[128,1,256]{2,1,0:T(1,128)S(1)} all-to-all(f32[128,1,256]{2,1,0:T(1,128)S(1)} %copy.105), channel_id=1, replica_groups=mesh['req'=4,'seq'=8] {'req'}, dimensions={0} | all-to-all | bytes 262144 | tf_op jit(solution)/shard_map/all_to_all | solution.py:174
  (105 shorter events, 18.6 us)
Async XLA Ops:
  21.0 1.2 copy-start.7
  21.0 1.2 copy-start.5
  41.5 0.7 copy-start.8
  48.5 1.2 copy-start.1
  48.5 7.9 %copy-start = (bf16[7,128,1024]{2,1,0:T(8,128)(2,1)}, bf16[7,128,1024]{2,1,0:T(8,128)(2,1)S(1)}, u32[]{:S(2)}) copy-start(bf16[7,128,1024]{2,1,0:T(8,128)(2,1)S(1)} %get-tuple-element.41) | copy-start | bytes 5505028
  54.5 1.2 copy-start.2
  57.0 1.2 copy-start.3
  62.7 5.9 %copy-start.4 = (bf16[4,8,4,256]{3,2,1,0:T(4,128)(2,1)S(1)}, bf16[4,8,4,256]{3,2,1,0:T(4,128)(2,1)}, u32[]{:S(2)}) copy-start(bf16[4,8,4,256]{3,2,1,0:T(4,128)(2,1)} %param.15) | copy-start | bytes 196612
  64.8 41.6 %all-to-all-start = ((f32[8,1,33280]{2,1,0:T(1,128)}), f32[8,1,33280]{2,1,0:T(1,128)S(1)}, u32[]{:S(2)}, u32[]{:S(2)}) async-start(f32[8,1,33280]{2,1,0:T(1,128)} %copy.101), calls=%async_computation | async-start | bytes 2129920 | tf_op jit(solution)/shard_map/all_to_all | solution.py:136
  68.3 126.3 %reduce-scatter.6.cloned.1.call-start = ((), (), s32[]{:S(2)}) async-start(), calls=%async_computation.7 | async-start | bytes 1187840 | tf_op jit(solution)/shard_map/reduce_scatter | solution.py:162
  85.4 20.9 %copy-start.6 = (f32[8192]{0:T(1024)S(1)}, f32[8192]{0:T(1024)}, u32[]{:S(2)}) copy-start(f32[8192]{0:T(1024)} %param.24) | copy-start | bytes 98308
  170.7 50.7 %reduce-scatter.4.cloned.1.call-start = ((), (), s32[]{:S(2)}) async-start(), calls=%async_computation.6 | async-start | bytes 1187840 | tf_op jit(solution)/shard_map/reduce_scatter | solution.py:161
  182.5 102.1 %reduce-scatter.8.cloned.1.call-start = ((), (), s32[]{:S(2)}) async-start(), calls=%async_computation.8 | async-start | bytes 589824 | tf_op jit(solution)/shard_map/reduce_scatter | solution.py:168
Sparse Core Ops, SparseCore 0:
  170.8 23.7 reduce-scatter.5
  197.0 24.3 reduce-scatter.3
  250.9 33.6 reduce-scatter.7
where the time goes:
time: 305 us; the launch traced here: 303 us
  blocking collectives  92.9 us (30%)
  waiting for transfers between devices  72.7 us (24%)
  matrix products  54.4 us (18%)
  local copies, waits for them, and re-layouts  51.7 us (17%)
  between operations  14.2 us (5%)
  other arithmetic  13 us (4%)
  starting transfers between devices  4.16 us (1%)
    reduce_scatter x1, waiting for transfers between devices, on_device(): lax.psum_scatter(down.reshape(down.shape[0], 1, quarter).astype(jnp.bfloa...  33.8 us
    reduce_scatter x1, waiting for transfers between devices, on_device(): lax.psum_scatter(gate_part, 'req', scatter_dimension=0, tiled=True)  26.8 us
    unnamed x35, local copies, waits for them, and re-layouts  22.2 us
    dot_general x1, local copies, waits for them, and re-layouts, on_device(): jnp.dot(attended, w_out.reshape(H * HD, blocks * pieces), preferred_eleme...  20.9 us
    all_to_all x1, blocking collectives, on_device(): lax.all_to_all(normed_mid, 'req', split_axis=1, concat_axis=0, tiled=True)  19.7 us
    all_gather x1, blocking collectives, on_device(): hidden = lax.all_gather(hidden_part, 'req', axis=0, tiled=True)  19.6 us
    reduce_scatter x1, waiting for transfers between devices, on_device(): up_sum = lax.psum_scatter(up_part, 'req', scatter_dimension=0, tiled=True)  12 us
    all_gather x1, blocking collectives, on_device(): lax.all_gather(hidden_in, 'seq', axis=3, tiled=True).reshape(rows, D)  11.7 us
  transfers between devices with their start and end apart: 4, of which 3 were waited for; matrix products, arithmetic and copies ran while one was open for 16% of the time, Pallas kernels for 0%

commit v1 on v0

--- a/solution.py
+++ b/solution.py
@@ -1,8 +1,11 @@
+import functools
 import math
 
 import jax
 import jax.numpy as jnp
 from jax import lax
+from jax.experimental import pallas as pl
+from jax.experimental.pallas import tpu as pltpu
 from jax.sharding import PartitionSpec as P
 
 D = 8192
@@ -28,6 +31,348 @@
     return jnp.concatenate(
         [first * cosine - second * sine, second * cosine + first * sine], axis=-1
     )
+
+
+MESH = pl.DeviceIdType.MESH
+
+
+def greet(partners):
+    barrier = pltpu.get_barrier_semaphore()
+    for partner in partners:
+        pl.semaphore_signal(barrier, inc=1, device_id=partner, device_id_type=MESH)
+    pl.semaphore_wait(barrier, len(partners))
+
+
+def remote(src, dst, send, recv, partner):
+    return pltpu.make_async_remote_copy(
+        src_ref=src,
+        dst_ref=dst,
+        send_sem=send,
+        recv_sem=recv,
+        device_id=partner,
+        device_id_type=MESH,
+    )
+
+
+def mlp_kernel(
+    zs,
+    ss,
+    width,
+    mid_ref,
+    norm_ref,
+    wg_hbm,
+    wu_hbm,
+    wd_hbm,
+    out_ref,
+    wg,
+    wu,
+    wd,
+    cut,
+    square,
+    got,
+    got_sq,
+    normed,
+    own_g,
+    own_u,
+    send_r,
+    recv_r,
+    send_l,
+    recv_l,
+    hid,
+    down,
+    parts,
+    landed,
+    sums,
+    back,
+    w_sem,
+    a_send,
+    a_recv,
+    b_send,
+    b_recv,
+    rs_send,
+    rs_recv,
+    ag_send,
+    ag_recv,
+    d_send,
+    d_recv,
+    e_send,
+    e_recv,
+):
+    z = lax.axis_index("req")
+    s = lax.axis_index("seq")
+    f32 = jnp.float32
+    rows = mid_ref.shape[0]
+    pieces = mid_ref.shape[1] // zs
+    units = wg.shape[1]
+    half = zs * rows // 2
+    loads = [
+        pltpu.make_async_copy(wg_hbm, wg, w_sem.at[0]),
+        pltpu.make_async_copy(wu_hbm, wu, w_sem.at[1]),
+        pltpu.make_async_copy(wd_hbm, wd, w_sem.at[2]),
+    ]
+    for load in loads:
+        load.start()
+    z_partners = [{"req": lax.rem(z + k, zs), "seq": s} for k in range(1, zs)]
+    s_partners = [{"req": z, "seq": lax.rem(s + k, ss)} for k in range(1, ss)]
+
+    total = jnp.zeros((8, rows), f32)
+    for block in range(zs):
+        piece = mid_ref[:, block * pieces : (block + 1) * pieces]
+        cut[block] = piece
+        value = piece.astype(f32)
+        total += lax.dot_general(
+            jnp.ones((8, pieces), f32),
+            value * value,
+            (((1,), (1,)), ((), ())),
+            precision=lax.Precision.HIGHEST,
+            preferred_element_type=f32,
+        )
+    square[...] = jnp.zeros_like(square)
+    square[:, :rows] = total
+    greet(z_partners + s_partners)
+    first = []
+    for k in range(1, zs):
+        to = lax.rem(z + k, zs)
+        first.append(
+            remote(cut.at[to], got.at[s, z], a_send.at[0, k], a_recv.at[0, k], z_partners[k - 1])
+        )
+        first.append(
+            remote(square, got_sq.at[s, z], a_send.at[1, k], a_recv.at[1, k], z_partners[k - 1])
+        )
+    for copy in first:
+        copy.start()
+    got[s, z] = cut[z]
+    got_sq[s, z] = square[...]
+    for copy in first:
+        copy.wait_recv()
+    second = []
+    for k in range(1, ss):
+        second.append(
+            remote(got.at[s], got.at[s], b_send.at[0, k], b_recv.at[0, k], s_partners[k - 1])
+        )
+        second.append(
+            remote(got_sq.at[s], got_sq.at[s], b_send.at[1, k], b_recv.at[1, k], s_partners[k - 1])
+        )
+    for copy in second:
+        copy.start()
+    for copy in second:
+        copy.wait_recv()
+    for group in range(zs):
+        line = got_sq[0, group]
+        for other in range(1, ss):
+            line = line + got_sq[other, group]
+        spread = lax.dot_general(
+            line[:, :rows],
+            jnp.full((8, 128), 0.125, f32),
+            (((0,), (0,)), ((), ())),
+            precision=lax.Precision.HIGHEST,
+            preferred_element_type=f32,
+        )
+        inverse = lax.rsqrt(spread / D + EPSILON)[:, :1]
+        for other in range(ss):
+            gain = norm_ref[:, other * pieces : (other + 1) * pieces]
+            normed[group * rows : (group + 1) * rows, other * pieces : (other + 1) * pieces] = (
+                got[other, group].astype(f32) * inverse * gain
+            ).astype(jnp.bfloat16)
+
+    starts = list(range(0, units, width))
+    count = len(starts)
+    sizes = [min(width, units - start) for start in starts]
+    padded = [-(-size // 128) * 128 for size in sizes]
+    if sizes[-1] != padded[-1]:
+        send_r[count - 1] = jnp.zeros_like(send_r[count - 1])
+        send_l[count - 1] = jnp.zeros_like(send_l[count - 1])
+        hid[count - 1] = jnp.zeros_like(hid[count - 1])
+    down[...] = jnp.zeros_like(down)
+    loads[0].wait()
+    loads[1].wait()
+
+    right = {"req": lax.rem(z + 1, zs), "seq": s}
+    left = {"req": lax.rem(z + zs - 1, zs), "seq": s}
+
+    def reduce_copy(way, p):
+        src, dst, to = ((send_r, recv_r, right), (send_l, recv_l, left))[way]
+        lanes = pl.ds(0, 2 * padded[p])
+        return remote(
+            src.at[p, :, lanes], dst.at[p, :, lanes], rs_send.at[way, p], rs_recv.at[way, p], to
+        )
+
+    def hidden_copy(way, p):
+        place = (p, pl.ds(half * (1 - way), half), pl.ds(0, padded[p]))
+        return remote(
+            hid.at[place],
+            hid.at[place],
+            ag_send.at[way, p],
+            ag_recv.at[way, p],
+            (left, right)[way],
+        )
+
+    def reduce_step(way, p, place):
+        size, pad = sizes[p], padded[p]
+        base = half * (1 - way)
+        cols = slice(starts[p], starts[p] + size)
+        gate = own_g[base : base + half, cols]
+        up = own_u[base : base + half, cols]
+        if place > 0:
+            reduce_copy(way, p).wait_recv()
+            came = (recv_r, recv_l)[way]
+            gate = gate + came[p, :, :size].astype(f32)
+            up = up + came[p, :, pad : pad + size].astype(f32)
+        if place < zs - 1:
+            goes = (send_r, send_l)[way]
+            goes[p, :, :size] = gate.astype(jnp.bfloat16)
+            goes[p, :, pad : pad + size] = up.astype(jnp.bfloat16)
+            reduce_copy(way, p).start()
+        else:
+            gate = gate.astype(jnp.bfloat16).astype(f32)
+            up = up.astype(jnp.bfloat16).astype(f32)
+            hid[p, base : base + half, :size] = (gate / (1.0 + jnp.exp(-gate)) * up).astype(
+                jnp.bfloat16
+            )
+            hidden_copy(way, p).start()
+
+    def down_step(p):
+        down[...] += jnp.dot(
+            hid[p, :, : sizes[p]],
+            wd[starts[p] : starts[p] + sizes[p], :],
+            preferred_element_type=f32,
+        )
+
+    lag = [0, 1, 3, 5, 7, 9, 11, 13, 15, 17]
+    last = lag[2 * zs - 2]
+    for i in range(count + last):
+        if i < count:
+            cols = slice(starts[i], starts[i] + sizes[i])
+            own_g[:, cols] = jnp.dot(normed[...], wg[:, cols], preferred_element_type=f32)
+            own_u[:, cols] = jnp.dot(normed[...], wu[:, cols], preferred_element_type=f32)
+        for zz in range(zs):
+
+            @pl.when(z == zz)
+            def _(zz=zz, i=i):
+                order = (0, 1) if zz < zs // 2 else (1, 0)
+                for way in order:
+                    place = zz if way == 0 else zs - 1 - zz
+                    p = i - lag[place]
+                    if 0 <= p < count:
+                        reduce_step(way, p, place)
+                for way in order[::-1]:
+                    place = zs - 1 - zz if way == 0 else zz
+                    p = i - lag[zs - 1 + place]
+                    if place > 0 and 0 <= p < count:
+                        hidden_copy(way, p).wait_recv()
+                        if place < zs - 1:
+                            hidden_copy(way, p).start()
+
+        if i == last:
+            loads[2].wait()
+        if i >= last:
+            down_step(i - last)
+
+    for other in range(ss):
+        parts[other] = down[:, other * pieces : (other + 1) * pieces].astype(jnp.bfloat16)
+    third = []
+    for k in range(1, ss):
+        to = lax.rem(s + k, ss)
+        third.append(
+            remote(parts.at[to], landed.at[s], d_send.at[k], d_recv.at[k], s_partners[k - 1])
+        )
+    for copy in third:
+        copy.start()
+    landed[s] = parts[s]
+    for copy in third:
+        copy.wait_recv()
+    whole = landed[0].astype(f32)
+    for other in range(1, ss):
+        whole = whole + landed[other].astype(f32)
+    for group in range(zs):
+        sums[group] = whole[group * rows : (group + 1) * rows]
+    fourth = []
+    for k in range(1, zs):
+        to = lax.rem(z + k, zs)
+        fourth.append(
+            remote(sums.at[to], back.at[z], e_send.at[k], e_recv.at[k], z_partners[k - 1])
+        )
+    for copy in fourth:
+        copy.start()
+    back[z] = sums[z]
+    for copy in fourth:
+        copy.wait_recv()
+    for block in range(zs):
+        cols = slice(block * pieces, (block + 1) * pieces)
+        out_ref[:, cols] = (mid_ref[:, cols].astype(f32) + back[block]).astype(jnp.bfloat16)
+
+    for copy in first + second + third + fourth:
+        copy.wait_send()
+    for way in range(2):
+        for p in range(count):
+
+            @pl.when(z != (zs - 1 if way == 0 else 0))
+            def _(way=way, p=p):
+                reduce_copy(way, p).wait_send()
+
+            @pl.when(z != (0 if way == 0 else zs - 1))
+            def _(way=way, p=p):
+                hidden_copy(way, p).wait_send()
+
+
+def mlp(middle, norm, w_gate, w_up, w_down, zs, ss):
+    rows, features = middle.shape
+    pieces = features // zs
+    depth, units = w_gate.shape
+    quarter = w_down.shape[1]
+    width = 512
+    count = -(-units // width)
+    everyone = zs * rows
+    half = everyone // 2
+    bf16, f32 = jnp.bfloat16, jnp.float32
+    vmem = pl.BlockSpec(memory_space=pltpu.VMEM)
+    hbm = pl.BlockSpec(memory_space=pl.ANY)
+    dma = pltpu.SemaphoreType.DMA
+    return pl.pallas_call(
+        functools.partial(mlp_kernel, zs, ss, width),
+        name="mlp",
+        out_shape=jax.ShapeDtypeStruct(middle.shape, bf16),
+        in_specs=[vmem, vmem, hbm, hbm, hbm],
+        out_specs=vmem,
+        scratch_shapes=[
+            pltpu.VMEM(w_gate.shape, bf16),
+            pltpu.VMEM(w_up.shape, bf16),
+            pltpu.VMEM(w_down.shape, bf16),
+            pltpu.VMEM((zs, rows, pieces), bf16),
+            pltpu.VMEM((8, 128), f32),
+            pltpu.VMEM((ss, zs, rows, pieces), bf16),
+            pltpu.VMEM((ss, zs, 8, 128), f32),
+            pltpu.VMEM((everyone, depth), bf16),
+            pltpu.VMEM((everyone, units), f32),
+            pltpu.VMEM((everyone, units), f32),
+            pltpu.VMEM((count, half, 2 * width), bf16),
+            pltpu.VMEM((count, half, 2 * width), bf16),
+            pltpu.VMEM((count, half, 2 * width), bf16),
+            pltpu.VMEM((count, half, 2 * width), bf16),
+            pltpu.VMEM((count, everyone, width), bf16),
+            pltpu.VMEM((everyone, quarter), f32),
+            pltpu.VMEM((ss, everyone, pieces), bf16),
+            pltpu.VMEM((ss, everyone, pieces), bf16),
+            pltpu.VMEM((zs, rows, pieces), f32),
+            pltpu.VMEM((zs, rows, pieces), f32),
+            dma((3,)),
+            dma((2, zs)),
+            dma((2, zs)),
+            dma((2, ss)),
+            dma((2, ss)),
+            dma((2, count)),
+            dma((2, count)),
+            dma((2, count)),
+            dma((2, count)),
+            dma((ss,)),
+            dma((ss,)),
+            dma((zs,)),
+            dma((zs,)),
+        ],
+        compiler_params=pltpu.CompilerParams(
+            collective_id=0, has_side_effects=True, vmem_limit_bytes=63 * 2**20
+        ),
+    )(middle, norm, w_gate, w_up, w_down)
 
 
 def on_device(
@@ -150,6 +495,19 @@
     ).reshape(rows, blocks, pieces)
     current = hidden_in.reshape(rows, blocks, pieces).astype(jnp.float32)
     middle = (current + branch_out).astype(jnp.bfloat16)
+    zs = D // w_gate.shape[0]
+    if pieces % 128 == 0 and zs == blocks and zs % 2 == 0 and rows <= 128 and rows % 16 == 0:
+        gain = lax.dynamic_slice(norm_mlp, (lax.axis_index("req") * quarter,), (quarter,))
+        output = mlp(
+            middle.reshape(rows, blocks * pieces),
+            gain.reshape(1, quarter),
+            w_gate,
+            w_up,
+            w_down,
+            zs,
+            seq,
+        )
+        return (output.reshape(hidden_in.shape), key_cache, value_cache)
     rows_mid = lax.all_gather(middle, "seq", axis=2, tiled=True).astype(jnp.float32)
     inverse = lax.rsqrt(jnp.mean(rows_mid * rows_mid, axis=(1, 2), keepdims=True) + EPSILON)
     normed_mid = (rows_mid * inverse * norm_mlp.reshape(blocks, quarter)).astype(jnp.bfloat16)

time: 305 us -> 241 us (0.79)
  Pallas kernels: 0 us -> 76.1 us
  waiting for transfers between devices: 72.7 us -> 0.01 us
  blocking collectives: 92.9 us -> 32.1 us
  local copies, waits for them, and re-layouts: 51.7 us -> 91.5 us
  matrix products: 54.4 us -> 23.2 us
  between operations: 14.2 us -> 1.08 us
    pallas_call x0 -> x1, Pallas kernels: none -> 76.1 us  [mlp(): pl.pallas_call(functools.partial(mlp_kernel, zs, ss, width), name='mlp',...]
    reduce_scatter x3 -> x0, waiting for transfers between devices: 72.7 us -> none  [the longest x1 33.8 us: on_device(): lax.psum_scatter(down.reshape(down.shape[0], 1, quarter).astype(jnp.bfloa...]
    unnamed x35 -> x34, local copies, waits for them, and re-layouts: 22.2 us -> 61 us
    dot_general x3 -> x0, matrix products: 31.3 us -> none  [the longest x1 11.5 us: on_device(): jnp.dot(mine, w_gate, preferred_element_type=jnp.float32)]
    all_gather x2 -> x0, blocking collectives: 30.9 us -> none  [the longest x1 19.6 us: on_device(): hidden = lax.all_gather(hidden_part, 'req', axis=0, tiled=True)]
    all_to_all x2 -> x0, blocking collectives: 30 us -> none  [the longest x1 19.7 us: on_device(): lax.all_to_all(normed_mid, 'req', split_axis=1, concat_axis=0, tiled=True)]
  transfers between devices with their start and end apart: 4 -> 1, of which waited for: 3 -> 0; matrix products, arithmetic and copies ran while one was open for 16% -> 32% of each run, Pallas kernels for 0% -> 0%
where the time goes in v1:
time: 241 us; the launch traced here: 239 us
  local copies, waits for them, and re-layouts  91.5 us (38%)
  Pallas kernels  76.1 us (32%)
  blocking collectives  32.1 us (13%)
  matrix products  23.2 us (10%)
  other arithmetic  11.3 us (5%)
  starting transfers between devices  3.78 us (2%)
    pallas_call x1, Pallas kernels, mlp(): pl.pallas_call(functools.partial(mlp_kernel, zs, ss, width), name='mlp',...  76.1 us
    unnamed x34, local copies, waits for them, and re-layouts  61 us
    dot_general x1, local copies, waits for them, and re-layouts, on_device(): jnp.dot(attended, w_out.reshape(H * HD, blocks * pieces), preferred_eleme...  20.9 us
    all_gather x1, blocking collectives, on_device(): lax.all_gather(hidden_in, 'seq', axis=3, tiled=True).reshape(rows, D)  11.7 us
    dot_general x1, matrix products, on_device(): jnp.dot(attended, w_out.reshape(H * HD, blocks * pieces), preferred_eleme...  10.8 us
    all_gather x1, blocking collectives, on_device(): projected = lax.all_gather(columns, 'seq', axis=1, tiled=True)  10.3 us
    all_gather x1, blocking collectives, on_device(): attended = lax.all_gather(heads, 'seq', axis=1, tiled=True)  10.1 us
    dot_general x1, matrix products, on_device(): jnp.dot(normed, w_qkv, preferred_element_type=jnp.float32)  8.95 us
  transfers between devices with their start and end apart: 1, of which 0 were waited for; matrix products, arithmetic and copies ran while one was open for 32% of the time, Pallas kernels for 0%

profile of v1, /device:TPU:0, one launch (start us, length us, event | category | flops | bytes accessed | tf_op | source)
XLA Modules:
  0.0 239.1 jit_solution(17912308211829780627)
XLA Ops:
  0.6 1.0 compare_reduce_fusion
  1.6 1.1 fusion.24
  2.7 11.7 %all_gather.9 = bf16[4,8,4,2048]{3,2,1,0:T(4,128)(2,1)S(1)} all-gather(bf16[4,8,4,256]{3,2,1,0:T(4,128)(2,1)} %param.15), channel_id=1, replica_groups=mesh['req'=4,'seq'=8] {'seq'}, dimensions={3}, use_global_device_ids=true | all-gather | bytes 589824 | tf_op jit(solution)/shard_map/all_gather | solution.py:417
  15.7 9.0 %fusion = bf16[32,1280]{1,0:T(8,128)(2,1)S(1)} fusion(bf16[8192,1280]{1,0:T(8,128)(2,1)} %param.21, f32[32,8192]{1,0:T(8,128)S(1)} %bitcast.109, f32[8192]{0:T(1024)S(1)} %copy-done.5, f32[32]{0:T(128)S(1)} %rsqrt.12, f32[1280]{0:T(1024)S(1)} %convert_element_type.60), kind=kOutput, calls=%fused_computation.5 | convolution fusion | flops 671956992 | bytes 22140032 | tf_op jit(solution)/shard_map/dot_general | solution.py:423
  24.7 10.3 %all_gather.10 = bf16[32,10240]{1,0:T(8,128)(2,1)S(1)} all-gather(bf16[32,1280]{1,0:T(8,128)(2,1)S(1)} %fusion), channel_id=1, replica_groups=mesh['req'=4,'seq'=8] {'seq'}, dimensions={1}, use_global_device_ids=true | all-gather | bytes 737280 | tf_op jit(solution)/shard_map/all_gather | solution.py:425
  39.1 2.8 %select_select_fusion = (bf16[7,128,1024]{2,1,0:T(8,128)(2,1)S(1)}, bf16[7,128,1024]{2,1,0:T(8,128)(2,1)S(1)}) fusion(bf16[7,128,1024]{2,1,0:T(8,128)(2,1)} %param.19, pred[7,128]{1,0:T(8,128)(4,1)S(1)} %get-tuple-element.46, pred[7,128]{1,0:T(8,128)(4,1)S(1)} %get-tuple-element.47, pred[7,128]{1,0:T(8,128)(4,1)S(1)} %get-tuple-element.48, ...), kind=kLoop, calls=%fused_computation.12 | loop fusion | flops 7340032 | bytes 7458304 | tf_op jit(solution)/shard_map/jit(_where)/select_n | solution.py:442
  42.5 0.7 copy-done.1
  43.2 1.4 bitcast_bitcast_fusion.1
  45.3 2.7 %fusion.39 = (f32[7,8,4,8]{3,2,1,0:T(4,128)S(1)}, f32[7,8,4,8,128]{4,3,2,1,0:T(8,128)S(1)}) fusion(bf16[7,128,8,128,1]{3,2,1,0,4:T(8,128)(2,1)} %bitcast_bitcast_fusion.1, pred[7,4,128]{2,1,0:T(4,128)(4,1)S(1)} %compare_and_fusion, bf16[7,4,8,8,128]{4,3,2,1,0:T(8,128)(2,1)S(1)} %gather_fusion, pred[7]{0:T(512)(128)(4,1)S(1)} %compare_and_fusion.1), kind=kOutput, calls=%fused_computation.103 | convolution fusion | flops 59635968 | bytes 3222023 | tf_op jit(solution)/shard_map/tjkgd,jpkd->jktgp/dot_general | solution.py:448
  48.0 0.7 convert_reduce_fusion
  50.6 1.0 copy-done.3
  51.6 0.7 fusion.1
  52.6 2.3 multiply_reduce_fusion
  56.2 2.1 copy.116
  58.3 3.8 %all-to-all-start = ((f32[8,1,33280]{2,1,0:T(1,128)}), f32[8,1,33280]{2,1,0:T(1,128)S(1)}, u32[]{:S(2)}, u32[]{:S(2)}) async-start(f32[8,1,33280]{2,1,0:T(1,128)} %copy.116), calls=%async_computation | async-start | bytes 2129920 | tf_op jit(solution)/shard_map/all_to_all | solution.py:481
  62.1 16.8 %copy.146 = bf16[1024,8,4,256]{3,1,2,0:T(8,128)(2,1)} copy(bf16[1024,8,4,256]{3,2,1,0:T(4,128)(2,1)} %bitcast.103) | data formatting | bytes 33554432
  78.9 20.9 %copy.119 = bf16[1024,8192]{1,0:T(8,128)(2,1)} copy(bf16[1024,8192]{0,1:T(8,128)(2,1)} %bitcast.102) | data formatting | bytes 33554432 | tf_op jit(solution)/shard_map/dot_general | solution.py:493
  99.8 19.1 %copy.121.wg_hbm = bf16[2048,3696]{1,0:T(8,128)(2,1)} copy(bf16[2048,3696]{0,1:T(8,128)(2,1)} %param.25) | data formatting | bytes 30277632 | tf_op args[10]
  118.8 19.0 %copy.122.wu_hbm = bf16[2048,3696]{1,0:T(8,128)(2,1)} copy(bf16[2048,3696]{0,1:T(8,128)(2,1)} %param.26) | data formatting | bytes 30277632 | tf_op args[11]
  137.8 1.3 dynamic_slice.3
  139.9 10.1 %all_gather.11 = bf16[32,8192]{1,0:T(8,128)(2,1)S(1)} all-gather(bf16[32,1024]{1,0:T(8,128)(2,1)S(1)} %copy_bitcast_fusion.2), channel_id=1, replica_groups=mesh['req'=4,'seq'=8] {'seq'}, dimensions={1}, use_global_device_ids=true | all-gather | bytes 589824 | tf_op jit(solution)/shard_map/all_gather | solution.py:492
  149.9 10.8 %fusion.12 = bf16[4,4,8,256]{3,2,1,0:T(8,128)(2,1)S(1)} fusion(bf16[4,256,8192]{2,1,0:T(8,128)(2,1)} %bitcast.101, bf16[32,8192]{1,0:T(8,128)(2,1)S(1)} %all_gather.11, f32[4,8,4,256]{3,2,1,0:T(4,128)S(1)} %convert_element_type.70), kind=kOutput, calls=%fused_computation.25 | convolution fusion | flops 536936448 | bytes 17498112 | tf_op jit(solution)/shard_map/dot_general | solution.py:493
  161.4 76.1 %mlp.1 = bf16[32,1024]{1,0:T(8,128)(2,1)} custom-call(bf16[32,1024]{1,0:T(8,128)(2,1)} %bitcast.120, f32[1,2048]{1,0:T(1,128)} %bitcast.130, bf16[2048,3696]{1,0:T(8,128)(2,1)} %copy.121.wg_hbm, bf16[2048,3696]{1,0:T(8,128)(2,1)} %copy.122.wu_hbm, bf16[3696,2048]{1,0:T(8,128)(2,1)} %wd_hbm.1), custom_call_target="tpu_custom_call" | custom-call | tf_op jit(solution)/shard_map/mlp/pallas_call | solution.py:331
  237.6 1.5 copy.123
  (84 shorter events, 11.3 us)
Async XLA Ops:
  14.5 1.2 copy-start.6
  14.5 1.2 copy-start.5
  35.0 0.7 copy-start.7
  41.9 1.2 copy-start.1
  42.0 7.9 %copy-start = (bf16[7,128,1024]{2,1,0:T(8,128)(2,1)}, bf16[7,128,1024]{2,1,0:T(8,128)(2,1)S(1)}, u32[]{:S(2)}) copy-start(bf16[7,128,1024]{2,1,0:T(8,128)(2,1)S(1)} %get-tuple-element.41) | copy-start | bytes 5505028
  48.0 1.2 copy-start.2
  50.4 1.2 copy-start.3
  56.1 5.9 %copy-start.4 = (bf16[4,8,4,256]{3,2,1,0:T(4,128)(2,1)S(1)}, bf16[4,8,4,256]{3,2,1,0:T(4,128)(2,1)}, u32[]{:S(2)}) copy-start(bf16[4,8,4,256]{3,2,1,0:T(4,128)(2,1)} %param.15) | copy-start | bytes 196612
  58.3 80.8 %all-to-all-start = ((f32[8,1,33280]{2,1,0:T(1,128)}), f32[8,1,33280]{2,1,0:T(1,128)S(1)}, u32[]{:S(2)}, u32[]{:S(2)}) async-start(f32[8,1,33280]{2,1,0:T(1,128)} %copy.116), calls=%async_computation | async-start | bytes 2129920 | tf_op jit(solution)/shard_map/all_to_all | solution.py:481

commit v2 on v1

--- a/solution.py
+++ b/solution.py
@@ -103,7 +103,7 @@
     f32 = jnp.float32
     rows = mid_ref.shape[0]
     pieces = mid_ref.shape[1] // zs
-    units = wg.shape[1]
+    units = wg.shape[0]
     half = zs * rows // 2
     loads = [
         pltpu.make_async_copy(wg_hbm, wg, w_sem.at[0]),
@@ -238,13 +238,14 @@
             preferred_element_type=f32,
         )
 
+    nt = (((1,), (1,)), ((), ()))
     lag = [0, 1, 3, 5, 7, 9, 11, 13, 15, 17]
     last = lag[2 * zs - 2]
     for i in range(count + last):
         if i < count:
             cols = slice(starts[i], starts[i] + sizes[i])
-            own_g[:, cols] = jnp.dot(normed[...], wg[:, cols], preferred_element_type=f32)
-            own_u[:, cols] = jnp.dot(normed[...], wu[:, cols], preferred_element_type=f32)
+            own_g[:, cols] = lax.dot_general(normed[...], wg[cols, :], nt, preferred_element_type=f32)
+            own_u[:, cols] = lax.dot_general(normed[...], wu[cols, :], nt, preferred_element_type=f32)
         for zz in range(zs):
 
             @pl.when(z == zz)
@@ -318,7 +319,7 @@
 def mlp(middle, norm, w_gate, w_up, w_down, zs, ss):
     rows, features = middle.shape
     pieces = features // zs
-    depth, units = w_gate.shape
+    units, depth = w_gate.shape
     quarter = w_down.shape[1]
     width = 512
     count = -(-units // width)
@@ -375,6 +376,248 @@
     )(middle, norm, w_gate, w_up, w_down)
 
 
+def project_kernel(
+    zs,
+    ss,
+    x_ref,
+    norm_ref,
+    bias_ref,
+    w_hbm,
+    out_ref,
+    w,
+    own,
+    got,
+    normed,
+    sent,
+    columns,
+    w_sem,
+    a_send,
+    a_recv,
+    b_send,
+    b_recv,
+):
+    z = lax.axis_index("req")
+    s = lax.axis_index("seq")
+    f32 = jnp.float32
+    rows, features = x_ref.shape
+    blocks = norm_ref.shape[0]
+    pieces = features // blocks
+    mine = w.shape[1]
+    parts = 4
+    depth = D // parts
+    loads = [
+        pltpu.make_async_copy(
+            w_hbm.at[pl.ds(part * depth, depth)], w.at[pl.ds(part * depth, depth)], w_sem.at[part]
+        )
+        for part in range(parts)
+    ]
+    for load in loads:
+        load.start()
+    partners = [{"req": z, "seq": lax.rem(s + k, ss)} for k in range(1, ss)]
+    own[...] = x_ref[...]
+    greet(partners)
+    first = [
+        remote(own, got.at[s], a_send.at[k], a_recv.at[k], partners[k - 1]) for k in range(1, ss)
+    ]
+    for copy in first:
+        copy.start()
+    got[s] = own[...]
+    for copy in first:
+        copy.wait_recv()
+    total = jnp.zeros((rows, 1), f32)
+    for other in range(ss):
+        value = got[other].astype(f32)
+        total += jnp.sum(value * value, axis=1, keepdims=True)
+    inverse = lax.rsqrt(total / D + EPSILON)
+    for other in range(ss):
+        for block in range(blocks):
+            lanes = slice(other * pieces, (other + 1) * pieces)
+            base = block * ss * pieces + other * pieces
+            value = got[other, :, block * pieces : (block + 1) * pieces].astype(f32)
+            normed[:, base : base + pieces] = (
+                value * inverse * norm_ref[block : block + 1, lanes]
+            ).astype(jnp.bfloat16)
+    result = jnp.zeros((rows, mine), f32)
+    for part in range(parts):
+        loads[part].wait()
+        span = slice(part * depth, (part + 1) * depth)
+        result += jnp.dot(normed[:, span], w[span, :], preferred_element_type=f32)
+    sent[...] = (result + bias_ref[...].astype(f32)).astype(jnp.bfloat16)
+    second = [
+        remote(sent, columns.at[s], b_send.at[k], b_recv.at[k], partners[k - 1])
+        for k in range(1, ss)
+    ]
+    for copy in second:
+        copy.start()
+    columns[s] = sent[...]
+    for copy in second:
+        copy.wait_recv()
+    for other in range(ss):
+        out_ref[:, other * mine : (other + 1) * mine] = columns[other]
+    for copy in first + second:
+        copy.wait_send()
+
+
+def project(x, norm, bias, w, zs, ss):
+    rows, features = x.shape
+    mine = w.shape[1]
+    bf16 = jnp.bfloat16
+    vmem = pl.BlockSpec(memory_space=pltpu.VMEM)
+    dma = pltpu.SemaphoreType.DMA
+    return pl.pallas_call(
+        functools.partial(project_kernel, zs, ss),
+        name="project",
+        out_shape=jax.ShapeDtypeStruct((rows, ss * mine), bf16),
+        in_specs=[vmem, vmem, vmem, pl.BlockSpec(memory_space=pl.ANY)],
+        out_specs=vmem,
+        scratch_shapes=[
+            pltpu.VMEM(w.shape, bf16),
+            pltpu.VMEM((rows, features), bf16),
+            pltpu.VMEM((ss, rows, features), bf16),
+            pltpu.VMEM((rows, D), bf16),
+            pltpu.VMEM((rows, mine), bf16),
+            pltpu.VMEM((ss, rows, mine), bf16),
+            dma((4,)),
+            dma((ss,)),
+            dma((ss,)),
+            dma((ss,)),
+            dma((ss,)),
+        ],
+        compiler_params=pltpu.CompilerParams(
+            collective_id=1, has_side_effects=True, vmem_limit_bytes=48 * 2**20
+        ),
+    )(x, norm, bias, w)
+
+
+def merge_kernel(
+    zs,
+    ss,
+    acc_ref,
+    stat_ref,
+    x_ref,
+    w_hbm,
+    out_ref,
+    w,
+    acc,
+    stat,
+    got,
+    got_stat,
+    heads,
+    everyone,
+    joined,
+    w_sem,
+    a_send,
+    a_recv,
+    b_send,
+    b_recv,
+):
+    z = lax.axis_index("req")
+    s = lax.axis_index("seq")
+    f32 = jnp.float32
+    rows = x_ref.shape[0]
+    per = H // ss
+    parts = 4
+    depth = D // parts
+    loads = [
+        pltpu.make_async_copy(
+            w_hbm.at[pl.ds(part * depth, depth)], w.at[pl.ds(part * depth, depth)], w_sem.at[part]
+        )
+        for part in range(parts)
+    ]
+    for load in loads:
+        load.start()
+    partners = [{"req": z, "seq": lax.rem(s + k, ss)} for k in range(1, ss)]
+    acc[...] = acc_ref[...]
+    stat[...] = stat_ref[...]
+    greet(partners)
+    first = []
+    for k in range(1, ss):
+        to = lax.rem(s + k, ss)
+        first.append(
+            remote(stat.at[to], got_stat.at[s], a_send.at[1, k], a_recv.at[1, k], partners[k - 1])
+        )
+        first.append(
+            remote(acc.at[to], got.at[s], a_send.at[0, k], a_recv.at[0, k], partners[k - 1])
+        )
+    for copy in first:
+        copy.start()
+    got[s] = acc[s]
+    got_stat[s] = stat[s]
+    for copy in first:
+        copy.wait_recv()
+    lines = per * rows // 128
+    best = got_stat[0, :lines]
+    for other in range(1, ss):
+        best = jnp.maximum(best, got_stat[other, :lines])
+    shares = [jnp.exp(got_stat[other, :lines] - best) for other in range(ss)]
+    denominator = shares[0] * got_stat[0, lines : 2 * lines]
+    for other in range(1, ss):
+        denominator = denominator + shares[other] * got_stat[other, lines : 2 * lines]
+    tall = jnp.transpose(
+        jnp.concatenate([share / denominator for share in shares], axis=0)
+    )
+    for line in range(lines):
+        span = slice(line * 128, (line + 1) * 128)
+        value = got[0, span, :] * tall[:, line : line + 1]
+        for other in range(1, ss):
+            at = other * lines + line
+            value = value + got[other, span, :] * tall[:, at : at + 1]
+        heads[span, :] = value.astype(jnp.bfloat16)
+    second = [
+        remote(heads, everyone.at[s], b_send.at[k], b_recv.at[k], partners[k - 1])
+        for k in range(1, ss)
+    ]
+    for copy in second:
+        copy.start()
+    everyone[s] = heads[...]
+    for copy in second:
+        copy.wait_recv()
+    for other in range(ss):
+        for head in range(per):
+            base = (other * per + head) * HD
+            joined[:, base : base + HD] = everyone[other, head * rows : (head + 1) * rows, :]
+    result = x_ref[...].astype(f32)
+    for part in range(parts):
+        loads[part].wait()
+        span = slice(part * depth, (part + 1) * depth)
+        result += jnp.dot(joined[:, span], w[span, :], preferred_element_type=f32)
+    out_ref[...] = result.astype(jnp.bfloat16)
+    for copy in first + second:
+        copy.wait_send()
+
+
+def merge(acc, stat, x, w, zs, ss):
+    rows, features = x.shape
+    bf16, f32 = jnp.bfloat16, jnp.float32
+    vmem = pl.BlockSpec(memory_space=pltpu.VMEM)
+    dma = pltpu.SemaphoreType.DMA
+    return pl.pallas_call(
+        functools.partial(merge_kernel, zs, ss),
+        name="merge",
+        out_shape=jax.ShapeDtypeStruct((rows, features), bf16),
+        in_specs=[vmem, vmem, vmem, pl.BlockSpec(memory_space=pl.ANY)],
+        out_specs=vmem,
+        scratch_shapes=[
+            pltpu.VMEM(w.shape, bf16),
+            pltpu.VMEM(acc.shape, f32),
+            pltpu.VMEM(stat.shape, f32),
+            pltpu.VMEM(acc.shape, f32),
+            pltpu.VMEM(stat.shape, f32),
+            pltpu.VMEM(acc.shape[1:], bf16),
+            pltpu.VMEM(acc.shape, bf16),
+            pltpu.VMEM((rows, H * HD), bf16),
+            dma((4,)),
+            dma((2, ss)),
+            dma((2, ss)),
+            dma((ss,)),
+            dma((ss,)),
+        ],
+        compiler_params=pltpu.CompilerParams(
+            collective_id=2, has_side_effects=True, vmem_limit_bytes=48 * 2**20
+        ),
+    )(acc, stat, x, w)
+
+
 def on_device(
     hidden_in,
     cache_lens,
@@ -397,6 +640,17 @@
     quarter = D // blocks
     seq = quarter // pieces
     scale = 1.0 / math.sqrt(HD)
+    zs = D // w_gate.shape[0]
+    fast = (
+        pieces % 128 == 0
+        and w_qkv.shape[1] % 128 == 0
+        and zs == blocks
+        and zs % 2 == 0
+        and rows <= 128
+        and rows % 16 == 0
+        and H % seq == 0
+        and (H // seq) * rows % 128 == 0
+    )
     slot_ids = lax.axis_index("seq") * slots + jnp.arange(slots, dtype=jnp.int32)
     matches = page_table[:, :, None] == slot_ids[None, None, :]
     live = jnp.any(matches, axis=(0, 1))
@@ -413,16 +667,26 @@
     slot_length = jnp.sum(jnp.where(owned, cache_lens[None, :], 0), axis=1)
     positions = logical[:, None] * per_page + jnp.arange(per_page, dtype=jnp.int32)[None, :]
 
-    flat = (
-        lax.all_gather(hidden_in, "seq", axis=3, tiled=True).reshape(rows, D).astype(jnp.float32)
-    )
-    normed = (
-        flat * lax.rsqrt(jnp.mean(flat * flat, axis=1, keepdims=True) + EPSILON) * norm_attn
-    ).astype(jnp.bfloat16)
-    columns = (
-        jnp.dot(normed, w_qkv, preferred_element_type=jnp.float32) + b_qkv.astype(jnp.float32)
-    ).astype(jnp.bfloat16)
-    projected = lax.all_gather(columns, "seq", axis=1, tiled=True)
+    if fast:
+        projected = project(
+            hidden_in.reshape(rows, blocks * pieces),
+            norm_attn.reshape(blocks, quarter),
+            b_qkv.reshape(1, -1),
+            w_qkv,
+            zs,
+            seq,
+        )
+    else:
+        flat = (
+            lax.all_gather(hidden_in, "seq", axis=3, tiled=True).reshape(rows, D).astype(jnp.float32)
+        )
+        normed = (
+            flat * lax.rsqrt(jnp.mean(flat * flat, axis=1, keepdims=True) + EPSILON) * norm_attn
+        ).astype(jnp.bfloat16)
+        columns = (
+            jnp.dot(normed, w_qkv, preferred_element_type=jnp.float32) + b_qkv.astype(jnp.float32)
+        ).astype(jnp.bfloat16)
+        projected = lax.all_gather(columns, "seq", axis=1, tiled=True)
     position = (
         jnp.arange(steps, dtype=jnp.int32)[:, None] + cache_lens[None, :]
     ).reshape(rows)
@@ -470,39 +734,49 @@
         value = jnp.swapaxes(value, 1, 2)
         return value.reshape((seq, H // seq, rows) + value.shape[4:])
 
-    packed = jnp.concatenate(
-        [
-            by_head(summed).reshape(seq, -1),
-            by_head(top).reshape(seq, -1),
-            by_head(total).reshape(seq, -1),
-        ],
-        axis=1,
-    )
-    packed = lax.all_to_all(packed, "seq", split_axis=0, concat_axis=0, tiled=True)
-    count = (H // seq) * rows
-    part_acc = packed[:, : count * HD].reshape(seq, count, HD)
-    part_top = packed[:, count * HD : count * (HD + 1)]
-    part_sum = packed[:, count * (HD + 1) :]
-    best = jnp.max(part_top, axis=0)
-    share = jnp.exp(part_top - best[None])
-    denominator = jnp.sum(share * part_sum, axis=0)
-    numerator = jnp.sum(share[..., None] * part_acc, axis=0)
-    heads = (numerator / denominator[:, None]).astype(jnp.bfloat16)
-    heads = jnp.swapaxes(heads.reshape(H // seq, rows, HD), 0, 1).reshape(rows, -1)
-    attended = lax.all_gather(heads, "seq", axis=1, tiled=True)
-    branch_out = jnp.dot(
-        attended, w_out.reshape(H * HD, blocks * pieces), preferred_element_type=jnp.float32
-    ).reshape(rows, blocks, pieces)
-    current = hidden_in.reshape(rows, blocks, pieces).astype(jnp.float32)
-    middle = (current + branch_out).astype(jnp.bfloat16)
-    zs = D // w_gate.shape[0]
-    if pieces % 128 == 0 and zs == blocks and zs % 2 == 0 and rows <= 128 and rows % 16 == 0:
+    if fast:
+        stat = jnp.concatenate([by_head(top), by_head(total)], axis=1).reshape(seq, -1, 128)
+        middle = merge(
+            by_head(summed).reshape(seq, -1, HD),
+            stat,
+            hidden_in.reshape(rows, blocks * pieces),
+            w_out.reshape(H * HD, blocks * pieces),
+            zs,
+            seq,
+        )
+    else:
+        packed = jnp.concatenate(
+            [
+                by_head(summed).reshape(seq, -1),
+                by_head(top).reshape(seq, -1),
+                by_head(total).reshape(seq, -1),
+            ],
+            axis=1,
+        )
+        packed = lax.all_to_all(packed, "seq", split_axis=0, concat_axis=0, tiled=True)
+        count = (H // seq) * rows
+        part_acc = packed[:, : count * HD].reshape(seq, count, HD)
+        part_top = packed[:, count * HD : count * (HD + 1)]
+        part_sum = packed[:, count * (HD + 1) :]
+        best = jnp.max(part_top, axis=0)
+        share = jnp.exp(part_top - best[None])
+        denominator = jnp.sum(share * part_sum, axis=0)
+        numerator = jnp.sum(share[..., None] * part_acc, axis=0)
+        heads = (numerator / denominator[:, None]).astype(jnp.bfloat16)
+        heads = jnp.swapaxes(heads.reshape(H // seq, rows, HD), 0, 1).reshape(rows, -1)
+        attended = lax.all_gather(heads, "seq", axis=1, tiled=True)
+        branch_out = jnp.dot(
+            attended, w_out.reshape(H * HD, blocks * pieces), preferred_element_type=jnp.float32
+        ).reshape(rows, blocks, pieces)
+        current = hidden_in.reshape(rows, blocks, pieces).astype(jnp.float32)
+        middle = (current + branch_out).astype(jnp.bfloat16)
+    if fast:
         gain = lax.dynamic_slice(norm_mlp, (lax.axis_index("req") * quarter,), (quarter,))
         output = mlp(
             middle.reshape(rows, blocks * pieces),
             gain.reshape(1, quarter),
-            w_gate,
-            w_up,
+            jnp.swapaxes(w_gate, 0, 1),
+            jnp.swapaxes(w_up, 0, 1),
             w_down,
             zs,
             seq,

time: 241 us -> 176 us (0.73)
  local copies, waits for them, and re-layouts: 91.5 us -> 32.2 us
  Pallas kernels: 76.1 us -> 126 us
  blocking collectives: 32.1 us -> 0 us
  matrix products: 23.2 us -> 3.38 us
  starting transfers between devices: 3.78 us -> 0 us
    pallas_call x0 -> x2, Pallas kernels: none -> 49.6 us  [the longest x1 26.2 us: merge(): pl.pallas_call(functools.partial(merge_kernel, zs, ss), name='merge', out...]
    unnamed x34 -> x26, local copies, waits for them, and re-layouts: 61 us -> 23.2 us
    all_gather x3 -> x0, blocking collectives: 32.1 us -> none  [the longest x1 11.7 us: on_device(): lax.all_gather(hidden_in, 'seq', axis=3, tiled=True).reshape(rows, D)]
    dot_general x1 -> x0, local copies, waits for them, and re-layouts: 20.9 us -> none  [on_device(): jnp.dot(attended, w_out.reshape(H * HD, blocks * pieces), preferred_eleme...]
    dot_general x2 -> x0, matrix products: 19.8 us -> none  [the longest x1 10.8 us: on_device(): jnp.dot(attended, w_out.reshape(H * HD, blocks * pieces), preferred_eleme...]
    all_to_all x1 -> x0, starting transfers between devices: 3.78 us -> none  [on_device(): lax.all_to_all(packed, 'seq', split_axis=0, concat_axis=0, tiled=True)]
  transfers between devices with their start and end apart: 1 -> 0, of which waited for: 0 -> 0; matrix products, arithmetic and copies ran while one was open for 32% -> 0% of each run, Pallas kernels for 0% -> 0%
where the time goes in v2:
time: 176 us; the launch traced here: 175 us
  Pallas kernels  126 us (72%)
  local copies, waits for them, and re-layouts  32.2 us (18%)
  other arithmetic  11.9 us (7%)
  matrix products  3.38 us (2%)
    pallas_call x1, Pallas kernels, mlp(): pl.pallas_call(functools.partial(mlp_kernel, zs, ss, width), name='mlp',...  76.7 us
    pallas_call x1, Pallas kernels, merge(): pl.pallas_call(functools.partial(merge_kernel, zs, ss), name='merge', out...  26.2 us
    pallas_call x1, Pallas kernels, project(): pl.pallas_call(functools.partial(project_kernel, zs, ss), name='project',...  23.4 us
    unnamed x26, local copies, waits for them, and re-layouts  23.2 us

profile of v2, /device:TPU:0, one launch (start us, length us, event | category | flops | bytes accessed | tf_op | source)
XLA Modules:
  0.0 174.9 jit_solution(351946765452783878)
XLA Ops:
  0.6 1.1 fusion.15
  1.7 1.0 compare_reduce_fusion
  2.7 0.8 select_reduce_fusion.1
  3.7 0.9 copy.79
  4.5 0.8 reshape.458.norm_ref
  5.3 0.7 reshape.459.bias_ref
  6.0 23.4 %project.1 = bf16[32,10240]{1,0:T(8,128)(2,1)S(1)} custom-call(bf16[32,1024]{1,0:T(8,128)(2,1)S(1)} %bitcast.72, f32[4,2048]{1,0:T(4,128)S(1)} %reshape.458.norm_ref, bf16[1,1280]{1,0:T(2,128)(2,1)S(1)} %reshape.459.bias_ref, bf16[8192,1280]{1,0:T(8,128)(2,1)} %w_hbm.1), custom_call_target="tpu_custom_call" | custom-call | tf_op jit(solution)/shard_map/project/pallas_call | solution.py:467
  32.8 3.0 %select_select_fusion.1 = (bf16[7,128,1024]{2,1,0:T(8,128)(2,1)S(1)}, bf16[7,128,1024]{2,1,0:T(8,128)(2,1)S(1)}) fusion(bf16[7,128,1024]{2,1,0:T(8,128)(2,1)} %param.18, pred[7,128]{1,0:T(8,128)(4,1)S(1)} %get-tuple-element.41, pred[7,128]{1,0:T(8,128)(4,1)S(1)} %get-tuple-element.42, pred[7,128]{1,0:T(8,128)(4,1)S(1)} %get-tuple-element.43, ...), kind=kLoop, calls=%fused_computation.11 | loop fusion | flops 7340032 | bytes 7458304 | tf_op jit(solution)/shard_map/jit(_where)/select_n | solution.py:705
  36.4 0.7 copy-done.1
  37.1 1.4 bitcast_bitcast_fusion.1
  38.7 1.1 fusion.12
  39.8 1.7 gather_fusion
  41.5 2.7 %fusion.29 = (f32[7,8,4,8]{3,2,1,0:T(4,128)S(1)}, f32[7,8,4,8,128]{4,3,2,1,0:T(8,128)S(1)}) fusion(bf16[7,128,8,128,1]{3,2,1,0,4:T(8,128)(2,1)} %bitcast_bitcast_fusion.1, pred[7,4,128]{2,1,0:T(4,128)(4,1)S(1)} %compare_and_fusion, bf16[7,4,8,8,128]{4,3,2,1,0:T(8,128)(2,1)S(1)} %gather_fusion, pred[7]{0:T(512)(128)(4,1)S(1)} %compare_and_fusion.1), kind=kOutput, calls=%fused_computation.79 | convolution fusion | flops 59635968 | bytes 3222023 | tf_op jit(solution)/shard_map/tjkgd,jpkd->jktgp/dot_general | solution.py:712
  44.2 0.7 convert_reduce_fusion
  47.1 1.0 copy-done.4
  48.2 0.7 fusion
  48.8 2.3 %multiply_reduce_fusion = f32[8,8,4,8,128]{4,3,2,1,0:T(8,128)S(1)} fusion(f32[7,8,4,8,128]{4,3,2,1,0:T(8,128)S(1)} %fusion, f32[7,8,8,4,8]{4,3,2,1,0:T(4,128)S(1)} %copy.57), kind=kLoop, calls=%fused_computation.3 | loop fusion | flops 3407872 | bytes 2023424 | tf_op jit(solution)/shard_map/reduce_sum | solution.py:731
  51.1 0.6 copy.60
  51.7 16.8 %copy.83 = bf16[1024,8,4,256]{3,1,2,0:T(8,128)(2,1)} copy(bf16[1024,8,4,256]{3,2,1,0:T(4,128)(2,1)} %bitcast.75) | data formatting | bytes 33554432
  68.5 26.2 %merge.1.mid_ref = bf16[32,1024]{1,0:T(8,128)(2,1)S(1)} custom-call(f32[8,256,128]{2,1,0:T(8,128)S(1)} %bitcast.71, f32[8,4,128]{2,1,0:T(4,128)S(1)} %reshape.467.stat_ref, bf16[32,1024]{1,0:T(8,128)(2,1)S(1)} %bitcast.73, bf16[8192,1024]{1,0:T(8,128)(2,1)} %bitcast.74), custom_call_target="tpu_custom_call" | custom-call | tf_op jit(solution)/shard_map/merge/pallas_call | solution.py:594
  94.7 0.6 copy-done
  95.3 1.3 dynamic_slice.3
  96.6 76.7 %mlp.1 = bf16[32,1024]{1,0:T(8,128)(2,1)} custom-call(bf16[32,1024]{1,0:T(8,128)(2,1)} %copy-done, f32[1,2048]{1,0:T(1,128)} %bitcast.96, bf16[3696,2048]{1,0:T(8,128)(2,1)} %bitcast.76, bf16[3696,2048]{1,0:T(8,128)(2,1)} %bitcast.77, bf16[3696,2048]{1,0:T(8,128)(2,1)} %wd_hbm.1), custom_call_target="tpu_custom_call" | custom-call | tf_op jit(solution)/shard_map/mlp/pallas_call | solution.py:332
  173.4 1.5 copy.64
  (60 shorter events, 6.3 us)
Async XLA Ops:
  29.4 0.7 copy-start.5
  35.8 1.2 copy-start.1
  35.8 10.6 %copy-start.2 = (bf16[7,128,1024]{2,1,0:T(8,128)(2,1)}, bf16[7,128,1024]{2,1,0:T(8,128)(2,1)S(1)}, u32[]{:S(2)}) copy-start(bf16[7,128,1024]{2,1,0:T(8,128)(2,1)S(1)} %get-tuple-element.37) | copy-start | bytes 5505028
  44.2 1.3 copy-start.3
  47.0 1.2 copy-start.4
  94.7 0.6 copy-start

commit v3 on v2

--- a/solution.py
+++ b/solution.py
@@ -239,7 +239,7 @@
         )
 
     nt = (((1,), (1,)), ((), ()))
-    lag = [0, 1, 3, 5, 7, 9, 11, 13, 15, 17]
+    lag = list(range(2 * zs))
     last = lag[2 * zs - 2]
     for i in range(count + last):
         if i < count:

time: 176 us -> 178 us (1.011)
  Pallas kernels: 126 us -> 129 us
    pallas_call x1, Pallas kernels: 76.7 us -> 79.3 us  [mlp(): pl.pallas_call(functools.partial(mlp_kernel, zs, ss, width), name='mlp',...]
where the time goes in v3:
time: 178 us; the launch traced here: 177 us
  Pallas kernels  129 us (72%)
  local copies, waits for them, and re-layouts  32.2 us (18%)
  other arithmetic  11.9 us (7%)
  matrix products  3.38 us (2%)
    pallas_call x1, Pallas kernels, mlp(): pl.pallas_call(functools.partial(mlp_kernel, zs, ss, width), name='mlp',...  79.3 us
    pallas_call x1, Pallas kernels, merge(): pl.pallas_call(functools.partial(merge_kernel, zs, ss), name='merge', out...  26.2 us
    pallas_call x1, Pallas kernels, project(): pl.pallas_call(functools.partial(project_kernel, zs, ss), name='project',...  23.4 us
    unnamed x26, local copies, waits for them, and re-layouts  23.2 us

profile of v3, /device:TPU:0, one launch (start us, length us, event | category | flops | bytes accessed | tf_op | source)
XLA Modules:
  0.0 177.5 jit_solution(13165899610843336055)
XLA Ops:
  0.6 1.1 fusion.15
  1.7 1.0 compare_reduce_fusion
  2.7 0.8 select_reduce_fusion.1
  3.7 0.9 copy.79
  4.5 0.8 reshape.458.norm_ref
  5.3 0.7 reshape.459.bias_ref
  6.0 23.4 %project.1 = bf16[32,10240]{1,0:T(8,128)(2,1)S(1)} custom-call(bf16[32,1024]{1,0:T(8,128)(2,1)S(1)} %bitcast.72, f32[4,2048]{1,0:T(4,128)S(1)} %reshape.458.norm_ref, bf16[1,1280]{1,0:T(2,128)(2,1)S(1)} %reshape.459.bias_ref, bf16[8192,1280]{1,0:T(8,128)(2,1)} %w_hbm.1), custom_call_target="tpu_custom_call" | custom-call | tf_op jit(solution)/shard_map/project/pallas_call | solution.py:467
  32.8 3.0 %select_select_fusion.1 = (bf16[7,128,1024]{2,1,0:T(8,128)(2,1)S(1)}, bf16[7,128,1024]{2,1,0:T(8,128)(2,1)S(1)}) fusion(bf16[7,128,1024]{2,1,0:T(8,128)(2,1)} %param.18, pred[7,128]{1,0:T(8,128)(4,1)S(1)} %get-tuple-element.41, pred[7,128]{1,0:T(8,128)(4,1)S(1)} %get-tuple-element.42, pred[7,128]{1,0:T(8,128)(4,1)S(1)} %get-tuple-element.43, ...), kind=kLoop, calls=%fused_computation.11 | loop fusion | flops 7340032 | bytes 7458304 | tf_op jit(solution)/shard_map/jit(_where)/select_n | solution.py:705
  36.4 0.7 copy-done.1
  37.1 1.4 bitcast_bitcast_fusion.1
  38.7 1.1 fusion.12
  39.8 1.7 gather_fusion
  41.5 2.7 %fusion.29 = (f32[7,8,4,8]{3,2,1,0:T(4,128)S(1)}, f32[7,8,4,8,128]{4,3,2,1,0:T(8,128)S(1)}) fusion(bf16[7,128,8,128,1]{3,2,1,0,4:T(8,128)(2,1)} %bitcast_bitcast_fusion.1, pred[7,4,128]{2,1,0:T(4,128)(4,1)S(1)} %compare_and_fusion, bf16[7,4,8,8,128]{4,3,2,1,0:T(8,128)(2,1)S(1)} %gather_fusion, pred[7]{0:T(512)(128)(4,1)S(1)} %compare_and_fusion.1), kind=kOutput, calls=%fused_computation.79 | convolution fusion | flops 59635968 | bytes 3222023 | tf_op jit(solution)/shard_map/tjkgd,jpkd->jktgp/dot_general | solution.py:712
  44.2 0.7 convert_reduce_fusion
  47.1 1.0 copy-done.4
  48.2 0.7 fusion
  48.8 2.3 %multiply_reduce_fusion = f32[8,8,4,8,128]{4,3,2,1,0:T(8,128)S(1)} fusion(f32[7,8,4,8,128]{4,3,2,1,0:T(8,128)S(1)} %fusion, f32[7,8,8,4,8]{4,3,2,1,0:T(4,128)S(1)} %copy.57), kind=kLoop, calls=%fused_computation.3 | loop fusion | flops 3407872 | bytes 2023424 | tf_op jit(solution)/shard_map/reduce_sum | solution.py:731
  51.1 0.6 copy.60
  51.7 16.8 %copy.83 = bf16[1024,8,4,256]{3,1,2,0:T(8,128)(2,1)} copy(bf16[1024,8,4,256]{3,2,1,0:T(4,128)(2,1)} %bitcast.75) | data formatting | bytes 33554432
  68.5 26.2 %merge.1.mid_ref = bf16[32,1024]{1,0:T(8,128)(2,1)S(1)} custom-call(f32[8,256,128]{2,1,0:T(8,128)S(1)} %bitcast.71, f32[8,4,128]{2,1,0:T(4,128)S(1)} %reshape.467.stat_ref, bf16[32,1024]{1,0:T(8,128)(2,1)S(1)} %bitcast.73, bf16[8192,1024]{1,0:T(8,128)(2,1)} %bitcast.74), custom_call_target="tpu_custom_call" | custom-call | tf_op jit(solution)/shard_map/merge/pallas_call | solution.py:594
  94.7 0.6 copy-done
  95.3 1.3 dynamic_slice.3
  96.6 79.3 %mlp.1 = bf16[32,1024]{1,0:T(8,128)(2,1)} custom-call(bf16[32,1024]{1,0:T(8,128)(2,1)} %copy-done, f32[1,2048]{1,0:T(1,128)} %bitcast.96, bf16[3696,2048]{1,0:T(8,128)(2,1)} %bitcast.76, bf16[3696,2048]{1,0:T(8,128)(2,1)} %bitcast.77, bf16[3696,2048]{1,0:T(8,128)(2,1)} %wd_hbm.1), custom_call_target="tpu_custom_call" | custom-call | tf_op jit(solution)/shard_map/mlp/pallas_call | solution.py:332
  176.0 1.5 copy.64
  (60 shorter events, 6.3 us)
Async XLA Ops:
  29.4 0.7 copy-start.5
  35.8 1.2 copy-start.1
  35.8 10.6 %copy-start.2 = (bf16[7,128,1024]{2,1,0:T(8,128)(2,1)}, bf16[7,128,1024]{2,1,0:T(8,128)(2,1)S(1)}, u32[]{:S(2)}) copy-start(bf16[7,128,1024]{2,1,0:T(8,128)(2,1)S(1)} %get-tuple-element.37) | copy-start | bytes 5505028
  44.2 1.3 copy-start.3
  47.0 1.2 copy-start.4
  94.7 0.6 copy-start
